TPU v7x, 256 devices: a whole 4x4x8 slice. The times are simulated.
256 devices in a mesh: pipe: 4 (over y_lo, core), ctx: 16 (over z, y_hi), tp: 4 (over x).
Axes of the slice: x: 4, y: 4 (y_hi: 2, y_lo: 2; y = y_hi * 2 + y_lo), z: 8, core: 2. Of those that a mesh axis runs over, the one named last changes fastest.
Arguments:
- segment_inputs: bfloat16 [4, 2, 2048, 4096], P('pipe', None, ('ctx', 'tp')), may hold values from -128 to 128
- keys: bfloat16 [4, 2, 2048, 512], P('pipe', None, 'ctx', 'tp'), may hold values from -64 to 64
- values: bfloat16 [4, 2, 2048, 512], P('pipe', None, 'ctx', 'tp'), may hold values from -6 to 6
- norm_gain: float32 [4, 4096], P('pipe'), may hold values from 0.1 to 1.9
- waiting_grads: bfloat16 [4, 2048, 4096], P('pipe', ('ctx', 'tp')), may hold values from -32 to 32
- output_grads: bfloat16 [1, 2048, 4096], P(None, ('ctx', 'tp')), may hold values from -32 to 32
- doc_lengths: int32 [5, 8], replicated, may hold values from 1 to 1024, as said below
Outputs:
- input_grads: bfloat16 [4, 2, 2048, 4096], P('pipe', None, ('ctx', 'tp'))
- key_grads: float32 [4, 2, 2048, 512], P('pipe', None, 'ctx', 'tp')
- value_grads: float32 [4, 2, 2048, 512], P('pipe', None, 'ctx', 'tp')
- gain_grads: float32 [4, 4096], P('pipe')
Inputs may be any that keep to these rules, and one draw needn't show every extreme that they name: `doc_lengths`: row m lists in order of position the lengths of the 8 documents packed into microbatch m's sequence; each row sums to 2048; the last document is exactly 1024 long.
All inputs are finite; a program needn't handle non-finite values.
Results may differ from a plain program's by a relative error of at most 0.009.
The roundings to bfloat16 on the way count: a program that leaves them out, or rounds other values in their place, can miss the bound.
Values may be sent and summed in bfloat16 or wider, within the bound.
A program may use at most 64 MiB of HBM per device.

v0:
```python
import jax
import jax.numpy as jnp
from jax import lax
from jax.sharding import PartitionSpec as P

HD = 128
S_DEV = 128
TICKS = 2
epsilon = 1e-05
masked_fill = -1e30


def passed_along(value, axis, by):
    count = lax.axis_size(axis)
    return lax.ppermute(value, axis, [(i, (i + by) % count) for i in range(count)])


def from_behind(value, axis, steps):
    count = lax.axis_size(axis)
    first, last = (max(0, -steps), min(count, count - steps))
    return lax.ppermute(value, axis, [(source, source + steps) for source in range(first, last)])


def row_positions(rows, half_rows, cycle_count):
    section = rows // half_rows
    offset = rows % half_rows
    owner = section // 2
    placed = jnp.where(section % 2 == 0, owner, 2 * cycle_count - 1 - owner)
    return placed * half_rows + offset


def document_starts(lengths_row, positions):
    closing = jnp.cumsum(lengths_row)
    passed = closing[None, :] <= positions[:, None]
    return jnp.sum(jnp.where(passed, lengths_row[None, :], 0), axis=1)


def keep_same(current):
    return current


def key_positions(key_first, key_count, cycle_count):
    rows = key_first + jnp.arange(key_count, dtype=jnp.int32)
    return row_positions(rows, S_DEV // 2, cycle_count)


def block_active(key_first, key_count, query_pos, query_start, cycle_count):
    key_pos = key_positions(key_first, key_count, cycle_count)
    return (jnp.min(key_pos) <= jnp.max(query_pos)) & (jnp.max(key_pos) >= jnp.min(query_start))


def score_block(query_block, key_block, query_pos, query_start, key_first, cycle_count):
    key_count = key_block.shape[0]
    key_pos = key_positions(key_first, key_count, cycle_count)
    scores = HD ** (-0.5) * jnp.einsum(
        "rkgd,skd->kgrs", query_block, key_block, preferred_element_type=jnp.float32
    )
    visible = (key_pos[None, :] <= query_pos[:, None]) & (key_pos[None, :] >= query_start[:, None])
    return (scores, visible[None, None])


def forward_update(carry, key_flat, value_flat, key_first, context):
    query_block, grad_block, query_pos, query_start, cycle_count = context
    key_count = key_flat.shape[0]

    def apply_block(current):
        row_peak, row_total, weighted = current
        key_block = key_flat.reshape(key_count, -1, HD)
        value_block = value_flat.reshape(key_count, -1, HD)
        scores, visible = score_block(
            query_block, key_block, query_pos, query_start, key_first, cycle_count
        )
        block_peak = jnp.max(jnp.where(visible, scores, masked_fill), axis=-1)
        new_peak = jnp.maximum(row_peak, block_peak)
        weights = jnp.where(visible, jnp.exp(scores - new_peak[..., None]), 0.0)
        prob_grad = jnp.einsum(
            "rkgd,skd->kgrs", grad_block, value_block, preferred_element_type=jnp.float32
        )
        return (new_peak, jnp.sum(weights, axis=-1), jnp.sum(weights * prob_grad, axis=-1))

    return lax.cond(
        block_active(key_first, key_count, query_pos, query_start, cycle_count),
        apply_block,
        keep_same,
        carry,
    )


def backward_terms(key_flat, value_flat, key_first, context, row_stats):
    query_block, grad_block, query_pos, query_start, cycle_count = context
    logsum, row_term = row_stats
    key_count = key_flat.shape[0]
    key_block = key_flat.reshape(key_count, -1, HD)
    value_block = value_flat.reshape(key_count, -1, HD)
    scale_factor = HD ** (-0.5)
    scores, visible = score_block(
        query_block, key_block, query_pos, query_start, key_first, cycle_count
    )
    prob_weights = jnp.where(visible, jnp.exp(scores - logsum[..., None]), 0.0)
    prob_grad = jnp.einsum(
        "rkgd,skd->kgrs", grad_block, value_block, preferred_element_type=jnp.float32
    )
    dscore = (prob_weights * (prob_grad - row_term[..., None])).astype(jnp.bfloat16)
    probs_low = prob_weights.astype(jnp.bfloat16)
    query_add = scale_factor * jnp.einsum(
        "kgrs,skd->rkgd", dscore, key_block, preferred_element_type=jnp.float32
    )
    key_add = scale_factor * jnp.einsum(
        "kgrs,rkgd->skd", dscore, query_block, preferred_element_type=jnp.float32
    )
    value_add = jnp.einsum(
        "kgrs,rkgd->skd", probs_low, grad_block, preferred_element_type=jnp.float32
    )
    return (query_add, key_add.reshape(key_count, -1), value_add.reshape(key_count, -1))


def segment_tick(inputs, key_local, value_local, gain_row, arriving, lengths_row):
    widened = inputs.astype(jnp.float32)
    inverse = lax.rsqrt(jnp.mean(widened * widened, axis=-1, keepdims=True) + epsilon)
    normed = widened * inverse
    queries = (normed * gain_row[None, :]).astype(jnp.bfloat16)
    query_heads, grad_heads = (
        lax.all_to_all(queries, "tp", split_axis=1, concat_axis=0, tiled=True),
        lax.all_to_all(arriving, "tp", split_axis=1, concat_axis=0, tiled=True),
    )
    row_count = key_local.shape[0]
    kv_local = key_local.shape[1] // HD
    group_size = query_heads.shape[1] // (HD * kv_local)
    query_block = query_heads.reshape(row_count, kv_local, group_size, HD)
    grad_block = grad_heads.reshape(row_count, kv_local, group_size, HD)
    cycle_count = lax.axis_size("ctx")
    cycle_place = lax.axis_index("ctx")
    query_pos = key_positions(cycle_place * row_count, row_count, cycle_count)
    query_start = document_starts(lengths_row, query_pos)
    context = (query_block, grad_block, query_pos, query_start, cycle_count)
    empty_peak = jnp.full((kv_local, group_size, row_count), masked_fill, jnp.float32)
    zero_rows = jnp.zeros((kv_local, group_size, row_count), jnp.float32)
    initial = (empty_peak, zero_rows, zero_rows)
    row_peak, row_total, weighted = forward_update(
        initial,
        lax.all_gather(key_local, "ctx", axis=0, tiled=True),
        lax.all_gather(value_local, "ctx", axis=0, tiled=True),
        jnp.int32(0),
        context,
    )
    row_stats = (row_peak + jnp.log(row_total), weighted / row_total)
    query_zero = jnp.zeros((row_count, kv_local, group_size, HD), jnp.float32)

    def cycle_turn(cycle_step, carry):
        key_block, value_block, key_grad, value_grad, query_grad = carry
        owner_index = (cycle_place - cycle_step) % cycle_count
        block_first = owner_index * row_count

        def apply_terms(current):
            added_terms = backward_terms(key_block, value_block, block_first, context, row_stats)
            return (
                current[0] + added_terms[1],
                current[1] + added_terms[2],
                current[2] + added_terms[0],
            )

        key_grad, value_grad, query_grad = lax.cond(
            block_active(block_first, row_count, query_pos, query_start, cycle_count),
            apply_terms,
            keep_same,
            (key_grad, value_grad, query_grad),
        )
        key_block, value_block = passed_along((key_block, value_block), "ctx", 1)
        key_grad, value_grad = passed_along((key_grad, value_grad), "ctx", 1)
        return (key_block, value_block, key_grad, value_grad, query_grad)

    zero_kv = jnp.zeros(key_local.shape, jnp.float32)
    finished = lax.fori_loop(
        0, cycle_count, cycle_turn, (key_local, value_local, zero_kv, zero_kv, query_zero)
    )
    key_grad, value_grad, query_grad = (finished[2], finished[3], finished[4])
    query_low = query_grad.reshape(row_count, -1).astype(jnp.bfloat16)
    grad_rows = lax.all_to_all(query_low, "tp", split_axis=0, concat_axis=1, tiled=True)
    rounded = grad_rows.astype(jnp.float32)
    scaled = rounded * gain_row[None, :]
    coupling = jnp.mean(scaled * normed, axis=-1, keepdims=True)
    input_grad = (arriving.astype(jnp.float32) + inverse * (scaled - normed * coupling)).astype(
        jnp.bfloat16
    )
    gain_part = jnp.sum(rounded * normed, axis=0)
    return (input_grad, key_grad, value_grad, gain_part)


def on_device(segment_inputs, keys, values, norm_gain, waiting_grads, output_grads, doc_lengths):
    segment_index = lax.axis_index("pipe")
    last_segment = lax.axis_size("pipe") - 1
    gain_row = norm_gain[0]
    arriving = waiting_grads[0]
    input_list = []
    key_list = []
    value_list = []
    gain_running = jnp.zeros(gain_row.shape, jnp.float32)
    for tick_index in range(TICKS):
        micro_index = segment_index + tick_index
        lengths_row = lax.dynamic_index_in_dim(doc_lengths, micro_index, 0, keepdims=False)
        input_grad, key_grad, value_grad, gain_part = segment_tick(
            segment_inputs[0, tick_index],
            keys[0, tick_index],
            values[0, tick_index],
            gain_row,
            arriving,
            lengths_row,
        )
        input_list.append(input_grad)
        key_list.append(key_grad)
        value_list.append(value_grad)
        gain_running = gain_running + gain_part
        if tick_index + 1 < TICKS:
            arrived = from_behind(input_grad, "pipe", -1)
            arriving = jnp.where(segment_index == last_segment, output_grads[tick_index], arrived)
    gain_grads = lax.psum(gain_running, ("ctx", "tp"))
    return (
        jnp.stack(input_list)[None],
        jnp.stack(key_list)[None],
        jnp.stack(value_list)[None],
        gain_grads[None],
    )


def solution(mesh):
    in_specs = (
        P("pipe", None, ("ctx", "tp"), None),
        P("pipe", None, "ctx", "tp"),
        P("pipe", None, "ctx", "tp"),
        P("pipe", None),
        P("pipe", ("ctx", "tp"), None),
        P(None, ("ctx", "tp"), None),
        P(),
    )
    out_specs = (
        P("pipe", None, ("ctx", "tp"), None),
        P("pipe", None, "ctx", "tp"),
        P("pipe", None, "ctx", "tp"),
        P("pipe", None),
    )
    return jax.shard_map(
        on_device, mesh=mesh, in_specs=in_specs, out_specs=out_specs, check_vma=False
    )
```

profile of v0, /device:TPU:8, one launch (start us, length us, event | category | flops | bytes accessed | tf_op | source)
XLA Modules:
  0.0 1165.9 jit_solution(12238675916187327474)
XLA Ops:
  6.3 4.3 all-to-all-start
  21.4 46.2 %all-gather = bf16[1,1,2048,128]{3,2,1,0:T(8,128)(2,1)S(1)} all-gather(bf16[1,1,128,128]{3,2,1,0:T(8,128)(2,1)S(1)} %get-tuple-element.1508), channel_id=2, replica_groups=mesh['pipe'=4,'ctx'=16,'tp'=4] {'ctx'}, dimensions={2}, use_global_device_ids=true | all-gather | bytes 557056 | tf_op jit(solution)/shard_map/all_gather | solution.py:141
  67.7 4.5 all-to-all-start.1
  72.2 40.6 %all-gather.1 = bf16[1,1,2048,128]{3,2,1,0:T(8,128)(2,1)} all-gather(bf16[1,1,128,128]{3,2,1,0:T(8,128)(2,1)S(1)} %get-tuple-element.1495), channel_id=3, replica_groups=mesh['pipe'=4,'ctx'=16,'tp'=4] {'ctx'}, dimensions={2}, use_global_device_ids=true | all-gather | bytes 557056 | tf_op jit(solution)/shard_map/all_gather | solution.py:142
  113.0 6.8 conditional.4
  120.0 273.9 %while.50 = (s32[]{:T(128)}, bf16[128,128]{1,0:T(8,128)(2,1)S(1)}, bf16[128,128]{1,0:T(8,128)(2,1)S(1)}, f32[128,128]{1,0:T(8,128)S(1)}, f32[128,128]{1,0:T(8,12...) while((s32[]{:T(128)}, bf16[128,128]{1,0:T(8,128)(2,1)S(1)}, ...), condition=%wide.region_17.18_spmd.clone, body=%wide.region_12.17_spmd.clone.sunk | while | flops 169071120 | bytes 6050608 | solution.py:173
  124.7 3.7 collective-permute-start.2
  133.1 3.2 collective-permute-done.3
  145.4 4.3 collective-permute-start.1
  159.8 3.5 collective-permute-start.3
  167.7 3.1 collective-permute-done
  182.6 3.1 collective-permute-done.2
  192.8 3.3 collective-permute-start.3
  198.5 3.0 collective-permute-start.1
  211.9 4.9 collective-permute-start.3
  219.8 4.8 collective-permute-done
  233.5 4.1 collective-permute-done.2
  245.1 3.3 collective-permute-start.3
  249.4 4.5 collective-permute-start.1
  264.2 2.7 collective-permute-start.3
  282.3 4.7 collective-permute-start.1
  297.2 2.9 collective-permute-start.3
  302.6 2.8 collective-permute-start.1
  315.6 2.8 collective-permute-start.3
  334.3 3.1 collective-permute-start.1
  347.7 4.5 collective-permute-start.3
  352.7 2.8 collective-permute-start.1
  355.6 4.1 collective-permute-done
  381.0 4.3 collective-permute-start.3
  386.3 4.7 collective-permute-start.1
  394.9 5.4 all-to-all-start.2
  400.3 6.7 all-to-all-done.2
  411.5 41.4 %all-gather.2 = bf16[1,1,2048,128]{3,2,1,0:T(8,128)(2,1)S(1)} all-gather(bf16[1,1,128,128]{3,2,1,0:T(8,128)(2,1)S(1)} %get-tuple-element.1505), channel_id=4, replica_groups=mesh['pipe'=4,'ctx'=16,'tp'=4] {'ctx'}, dimensions={2}, use_global_device_ids=true | all-gather | bytes 557056 | tf_op jit(solution)/shard_map/all_gather | solution.py:141
  454.9 41.8 %all-gather.3 = bf16[1,1,2048,128]{3,2,1,0:T(8,128)(2,1)} all-gather(bf16[1,1,128,128]{3,2,1,0:T(8,128)(2,1)S(1)} %get-tuple-element.1492), channel_id=5, replica_groups=mesh['pipe'=4,'ctx'=16,'tp'=4] {'ctx'}, dimensions={2}, use_global_device_ids=true | all-gather | bytes 557056 | tf_op jit(solution)/shard_map/all_gather | solution.py:142
  496.7 3.4 all-to-all-start.3
  502.7 4.1 all-to-all-done.3
  506.8 4.0 all-to-all-start.4
  512.4 5.1 all-to-all-done.4
  518.6 6.9 conditional.5
  525.6 273.6 %while.51 = (s32[]{:T(128)}, bf16[128,128]{1,0:T(8,128)(2,1)S(1)}, bf16[128,128]{1,0:T(8,128)(2,1)S(1)}, f32[128,128]{1,0:T(8,128)S(1)}, f32[128,128]{1,0:T(8,12...) while((s32[]{:T(128)}, bf16[128,128]{1,0:T(8,128)(2,1)S(1)}, ...), condition=%wide.region_33.34_spmd.clone, body=%wide.region_28.33_spmd.clone.sunk | while | flops 169071120 | bytes 6050608 | solution.py:173
  535.4 3.6 collective-permute-done.6
  550.4 4.7 collective-permute-start.5
  562.7 2.7 collective-permute-start.6
  567.5 3.6 collective-permute-start.4
  575.0 3.6 collective-permute-done.5
  587.4 3.9 collective-permute-done.6
  603.3 3.1 collective-permute-start.5
  616.8 4.9 collective-permute-start.7
  624.7 4.5 collective-permute-done.4
  638.8 3.5 collective-permute-done.6
  650.0 4.1 collective-permute-start.7
  655.0 4.7 collective-permute-start.5
  667.4 2.7 collective-permute-start.6
  670.0 2.6 collective-permute-start.7
  688.3 3.7 collective-permute-start.5
  702.3 3.1 collective-permute-start.7
  740.2 3.1 collective-permute-start.5
  753.7 4.9 collective-permute-start.7
  761.6 4.5 collective-permute-done.4
  786.8 3.7 collective-permute-start.7
  791.7 4.7 collective-permute-start.5
  800.3 3.4 all-to-all-start.5
  805.0 5.3 all-to-all-done.5
  810.8 353.9 %psum.7 = f32[1,4096]{1,0:T(1,128)} all-reduce(f32[1,4096]{1,0:T(1,128)S(1)} %bitcast.426), channel_id=1, replica_groups=mesh['pipe'=4,'ctx'=16,'tp'=4] {'ctx','tp'}, use_global_device_ids=true, to_apply=%region_37.38 | all-reduce | flops 4096 | bytes 32768 | tf_op jit(solution)/shard_map/psum | solution.py:216
  (956 shorter events, 382.2 us)
Async XLA Ops:
  6.3 61.3 %all-to-all-start = ((bf16[32,4,1024]{2,0,1:T(8,128)(2,1)}), bf16[32,4,1024]{2,0,1:T(8,128)(2,1)S(1)}, u32[]{:S(2)}, u32[]{:S(2)}) async-start(bf16[32,4,1024]{2,0,1:T(8,128)(2,1)} %multiply_convert_fusion.1), calls=%async_computation | async-start | bytes 524288 | tf_op jit(solution)/shard_map/all_to_all | solution.py:123
  67.7 45.2 %all-to-all-start.1 = ((bf16[32,4,1024]{2,0,1:T(8,128)(2,1)}), bf16[32,4,1024]{2,0,1:T(8,128)(2,1)S(1)}, u32[]{:S(2)}, u32[]{:S(2)}) async-start(bf16[32,4,1024]{2,0,1:T(8,128)(2,1)} %copy.84), calls=%async_computation.1 | async-start | bytes 524288 | tf_op jit(solution)/shard_map/all_to_all | solution.py:124
  124.7 8.4 collective-permute-start.2
  128.6 8.2 collective-permute-start
  143.0 8.3 collective-permute-start.2
  143.1 9.3 collective-permute-start.3
  144.4 8.3 collective-permute-start
  157.8 9.0 collective-permute-start.2
  177.7 8.0 collective-permute-start.2
  177.8 8.6 collective-permute-start.3
  192.7 8.8 collective-permute-start.2
  192.8 8.7 collective-permute-start.3
  210.7 8.1 collective-permute-start.2
  216.8 8.1 collective-permute-start.1
  229.7 8.0 collective-permute-start.2
  229.7 8.7 collective-permute-start.3
  232.2 8.1 collective-permute-start.1
  245.0 9.0 collective-permute-start.2
  245.1 8.9 collective-permute-start.3
  261.7 8.4 collective-permute-start.2
  267.0 8.1 collective-permute-start.1
  279.8 8.6 collective-permute-start.2
  279.8 9.8 collective-permute-start.3
  281.5 8.5 collective-permute-start
  282.3 8.0 collective-permute-start.1
  295.0 10.4 collective-permute-start.2
  297.2 8.2 collective-permute-start.3
  331.1 8.6 collective-permute-start.3
  346.5 9.0 collective-permute-start.2
  380.8 10.3 collective-permute-start.2
  381.0 10.1 collective-permute-start.3
  394.9 12.0 %all-to-all-start.2 = ((bf16[4,32,1024]{2,1,0:T(8,128)(2,1)}), bf16[4,32,1024]{2,1,0:T(8,128)(2,1)S(1)}, u32[]{:S(2)}, u32[]{:S(2)}) async-start(bf16[4,32,1024]{2,1,0:T(8,128)(2,1)} %convert_element_type.172), calls=%async_computation.2 | async-start | bytes 524288 | tf_op jit(solution)/shard_map/all_to_all | solution.py:178
  409.6 91.3 %collective-permute-start.8 = (bf16[32,4096]{1,0:T(8,128)(2,1)}, bf16[32,4096]{1,0:T(8,128)(2,1)}, u32[]{:S(2)}, u32[]{:S(2)}) collective-permute-start(bf16[32,4096]{1,0:T(8,128)(2,1)} %fusion.122), channel_id=1, source_target_pairs={{64,0},{128,64},{192,128},{65,1},{129,65},{193,129},{66,2},{130,66... | collective-permute-start | bytes 786440 | tf_op jit(solution)/shard_map/ppermute | solution.py:21
  496.7 10.1 all-to-all-start.3
  506.8 10.8 all-to-all-start.4
  530.4 8.6 collective-permute-start.6
  533.1 8.1 collective-permute-start.4
  547.6 8.1 collective-permute-start.6
  547.7 8.7 collective-permute-start.7
  562.7 9.6 collective-permute-start.6
  583.4 8.6 collective-permute-start.7
  598.3 8.1 collective-permute-start.6
  598.4 8.6 collective-permute-start.7
  615.6 8.7 collective-permute-start.6
  634.6 8.5 collective-permute-start.7
  636.8 8.3 collective-permute-start.5
  649.9 9.8 collective-permute-start.6
  650.0 9.8 collective-permute-start.7
  667.4 8.1 collective-permute-start.6
  670.0 8.0 collective-permute-start.7
  685.3 8.3 collective-permute-start.6
  685.4 8.9 collective-permute-start.7
  700.6 9.8 collective-permute-start.6
  702.3 8.1 collective-permute-start.7
  720.2 8.0 collective-permute-start.6
  720.6 8.2 collective-permute-start.7
  735.9 8.0 collective-permute-start.6
  736.2 8.4 collective-permute-start.7
  752.5 8.8 collective-permute-start.6
  771.2 8.0 collective-permute-start.6
  771.6 8.3 collective-permute-start.7
  786.7 9.7 collective-permute-start.6
  786.8 9.6 collective-permute-start.7
  800.3 10.1 all-to-all-start.5
  (82 other events, 3647.2 us)
where the time goes:
time: 1170 us
  blocking collectives  524 us (45%)
  starting transfers between devices  263 us (22%)
  waiting for transfers between devices  180 us (15%)
  loops' own time  85 us (7%)
  other arithmetic  51.5 us (4%)
  matrix products  46.7 us (4%)
    psum x1, blocking collectives, on_device(): gain_grads = lax.psum(gain_running, ('ctx', 'tp'))  354 us
    ppermute x128, starting transfers between devices, passed_along(): lax.ppermute(value, axis, [(i, (i + by) % count) for i in range(count)])  236 us
    ppermute x128, waiting for transfers between devices, passed_along(): lax.ppermute(value, axis, [(i, (i + by) % count) for i in range(count)])  159 us
    all_gather x2, blocking collectives, segment_tick(): lax.all_gather(key_local, 'ctx', axis=0, tiled=True)  87.6 us
    all_gather x2, blocking collectives, segment_tick(): lax.all_gather(value_local, 'ctx', axis=0, tiled=True)  82.4 us
    another operation x2, loops' own time, segment_tick(): lax.fori_loop(0, cycle_count, cycle_turn, (key_local, value_local, zero_k...  82.4 us
    reduce_max x33, other arithmetic, block_active(): jnp.max(key_pos) >= jnp.min(query_start)  23.7 us
  transfers between devices with their start and end apart: 135, of which 110 were waited for; matrix products, arithmetic and copies ran while one was open for 1% of the time, Pallas kernels for 0%

commit v1 on v0

--- a/solution.py
+++ b/solution.py
@@ -213,7 +213,7 @@
         if tick_index + 1 < TICKS:
             arrived = from_behind(input_grad, "pipe", -1)
             arriving = jnp.where(segment_index == last_segment, output_grads[tick_index], arrived)
-    gain_grads = lax.psum(gain_running, ("ctx", "tp"))
+    gain_grads = lax.psum(lax.psum(gain_running, "ctx"), "tp")
     return (
         jnp.stack(input_list)[None],
         jnp.stack(key_list)[None],

time: 1170 us -> 904 us (0.77)
  blocking collectives: 524 us -> 260 us
    psum x1 -> x2, blocking collectives: 354 us -> 90.3 us  [on_device(): gain_grads = lax.psum(lax.psum(gain_running, 'ctx'), 'tp')]
  transfers between devices with their start and end apart: 135 -> 135, of which waited for: 110 -> 110; matrix products, arithmetic and copies ran while one was open for 1% -> 2% of each run, Pallas kernels for 0% -> 0%
where the time goes in v1:
time: 904 us; the launch traced here: 902 us
  starting transfers between devices  263 us (29%)
  blocking collectives  260 us (29%)
  waiting for transfers between devices  180 us (20%)
  loops' own time  85 us (9%)
  other arithmetic  51.5 us (6%)
  matrix products  46.7 us (5%)
  local copies, waits for them, and re-layouts  10.6 us (1%)
    ppermute x128, starting transfers between devices, passed_along(): lax.ppermute(value, axis, [(i, (i + by) % count) for i in range(count)])  236 us
    ppermute x128, waiting for transfers between devices, passed_along(): lax.ppermute(value, axis, [(i, (i + by) % count) for i in range(count)])  159 us
    psum x2, blocking collectives, on_device(): gain_grads = lax.psum(lax.psum(gain_running, 'ctx'), 'tp')  90.3 us
    all_gather x2, blocking collectives, segment_tick(): lax.all_gather(key_local, 'ctx', axis=0, tiled=True)  87.6 us
    all_gather x2, blocking collectives, segment_tick(): lax.all_gather(value_local, 'ctx', axis=0, tiled=True)  82.4 us
    another operation x2, loops' own time, segment_tick(): lax.fori_loop(0, cycle_count, cycle_turn, (key_local, value_local, zero_k...  82.4 us
    reduce_max x33, other arithmetic, block_active(): jnp.max(key_pos) >= jnp.min(query_start)  23.7 us
  transfers between devices with their start and end apart: 135, of which 110 were waited for; matrix products, arithmetic and copies ran while one was open for 2% of the time, Pallas kernels for 0%

profile of v1, /device:TPU:8, one launch (start us, length us, event | category | flops | bytes accessed | tf_op | source)
XLA Modules:
  0.0 902.3 jit_solution(13295326929773803791)
XLA Ops:
  6.3 4.3 all-to-all-start
  21.4 46.2 %all-gather = bf16[1,1,2048,128]{3,2,1,0:T(8,128)(2,1)S(1)} all-gather(bf16[1,1,128,128]{3,2,1,0:T(8,128)(2,1)S(1)} %get-tuple-element.1508), channel_id=2, replica_groups=mesh['pipe'=4,'ctx'=16,'tp'=4] {'ctx'}, dimensions={2}, use_global_device_ids=true | all-gather | bytes 557056 | tf_op jit(solution)/shard_map/all_gather | solution.py:141
  67.7 4.5 all-to-all-start.1
  72.2 40.6 %all-gather.1 = bf16[1,1,2048,128]{3,2,1,0:T(8,128)(2,1)} all-gather(bf16[1,1,128,128]{3,2,1,0:T(8,128)(2,1)S(1)} %get-tuple-element.1495), channel_id=3, replica_groups=mesh['pipe'=4,'ctx'=16,'tp'=4] {'ctx'}, dimensions={2}, use_global_device_ids=true | all-gather | bytes 557056 | tf_op jit(solution)/shard_map/all_gather | solution.py:142
  113.0 6.8 conditional.4
  120.0 273.9 %while.50 = (s32[]{:T(128)}, bf16[128,128]{1,0:T(8,128)(2,1)S(1)}, bf16[128,128]{1,0:T(8,128)(2,1)S(1)}, f32[128,128]{1,0:T(8,128)S(1)}, f32[128,128]{1,0:T(8,12...) while((s32[]{:T(128)}, bf16[128,128]{1,0:T(8,128)(2,1)S(1)}, ...), condition=%wide.region_17.18_spmd.clone, body=%wide.region_12.17_spmd.clone.sunk | while | flops 169071120 | bytes 6050608 | solution.py:173
  124.7 3.7 collective-permute-start.2
  133.1 3.2 collective-permute-done.3
  145.4 4.3 collective-permute-start.1
  159.8 3.5 collective-permute-start.3
  167.7 3.1 collective-permute-done
  182.6 3.1 collective-permute-done.2
  192.8 3.3 collective-permute-start.3
  198.5 3.0 collective-permute-start.1
  211.9 4.9 collective-permute-start.3
  219.8 4.8 collective-permute-done
  233.5 4.1 collective-permute-done.2
  245.1 3.3 collective-permute-start.3
  249.4 4.5 collective-permute-start.1
  264.2 2.7 collective-permute-start.3
  282.3 4.7 collective-permute-start.1
  297.2 2.9 collective-permute-start.3
  302.6 2.8 collective-permute-start.1
  315.6 2.8 collective-permute-start.3
  334.3 3.1 collective-permute-start.1
  347.7 4.5 collective-permute-start.3
  352.7 2.8 collective-permute-start.1
  355.6 4.1 collective-permute-done
  381.0 4.3 collective-permute-start.3
  386.3 4.7 collective-permute-start.1
  394.9 5.4 all-to-all-start.2
  400.3 6.7 all-to-all-done.2
  411.5 41.4 %all-gather.2 = bf16[1,1,2048,128]{3,2,1,0:T(8,128)(2,1)S(1)} all-gather(bf16[1,1,128,128]{3,2,1,0:T(8,128)(2,1)S(1)} %get-tuple-element.1505), channel_id=4, replica_groups=mesh['pipe'=4,'ctx'=16,'tp'=4] {'ctx'}, dimensions={2}, use_global_device_ids=true | all-gather | bytes 557056 | tf_op jit(solution)/shard_map/all_gather | solution.py:141
  454.9 41.8 %all-gather.3 = bf16[1,1,2048,128]{3,2,1,0:T(8,128)(2,1)} all-gather(bf16[1,1,128,128]{3,2,1,0:T(8,128)(2,1)S(1)} %get-tuple-element.1492), channel_id=5, replica_groups=mesh['pipe'=4,'ctx'=16,'tp'=4] {'ctx'}, dimensions={2}, use_global_device_ids=true | all-gather | bytes 557056 | tf_op jit(solution)/shard_map/all_gather | solution.py:142
  496.7 3.4 all-to-all-start.3
  502.7 4.1 all-to-all-done.3
  506.8 4.0 all-to-all-start.4
  512.4 5.1 all-to-all-done.4
  518.6 6.9 conditional.5
  525.6 273.6 %while.51 = (s32[]{:T(128)}, bf16[128,128]{1,0:T(8,128)(2,1)S(1)}, bf16[128,128]{1,0:T(8,128)(2,1)S(1)}, f32[128,128]{1,0:T(8,128)S(1)}, f32[128,128]{1,0:T(8,12...) while((s32[]{:T(128)}, bf16[128,128]{1,0:T(8,128)(2,1)S(1)}, ...), condition=%wide.region_33.34_spmd.clone, body=%wide.region_28.33_spmd.clone.sunk | while | flops 169071120 | bytes 6050608 | solution.py:173
  535.4 3.6 collective-permute-done.6
  550.4 4.7 collective-permute-start.5
  562.7 2.7 collective-permute-start.6
  567.5 3.6 collective-permute-start.4
  575.0 3.6 collective-permute-done.5
  587.4 3.9 collective-permute-done.6
  603.3 3.1 collective-permute-start.5
  616.8 4.9 collective-permute-start.7
  624.7 4.5 collective-permute-done.4
  638.8 3.5 collective-permute-done.6
  650.0 4.1 collective-permute-start.7
  655.0 4.7 collective-permute-start.5
  667.4 2.7 collective-permute-start.6
  688.3 3.7 collective-permute-start.5
  702.3 3.1 collective-permute-start.7
  740.2 3.1 collective-permute-start.5
  753.7 4.9 collective-permute-start.7
  761.6 4.5 collective-permute-done.4
  786.8 3.7 collective-permute-start.7
  791.7 4.8 collective-permute-start.5
  800.3 3.4 all-to-all-start.5
  805.0 5.3 all-to-all-done.5
  810.8 74.4 %psum.14 = f32[4096]{0:T(1024)S(1)} all-reduce(f32[4096]{0:T(1024)S(1)} %bitcast.428), channel_id=1, replica_groups=mesh['pipe'=4,'ctx'=16,'tp'=4] {'ctx'}, use_global_device_ids=true, to_apply=%region_37.38 | all-reduce | flops 4096 | bytes 32768 | tf_op jit(solution)/shard_map/psum | solution.py:216
  885.2 15.9 %psum.15 = f32[1,4096]{1,0:T(1,128)} all-reduce(f32[1,4096]{1,0:T(1,128)S(1)} %bitcast.429), channel_id=1, replica_groups=mesh['pipe'=4,'ctx'=16,'tp'=4] {'tp'}, use_global_device_ids=true, to_apply=%region_38.39 | all-reduce | flops 4096 | bytes 32768 | tf_op jit(solution)/shard_map/psum | solution.py:216
  (957 shorter events, 384.8 us)
Async XLA Ops:
  6.3 61.3 %all-to-all-start = ((bf16[32,4,1024]{2,0,1:T(8,128)(2,1)}), bf16[32,4,1024]{2,0,1:T(8,128)(2,1)S(1)}, u32[]{:S(2)}, u32[]{:S(2)}) async-start(bf16[32,4,1024]{2,0,1:T(8,128)(2,1)} %multiply_convert_fusion.1), calls=%async_computation | async-start | bytes 524288 | tf_op jit(solution)/shard_map/all_to_all | solution.py:123
  67.7 45.2 %all-to-all-start.1 = ((bf16[32,4,1024]{2,0,1:T(8,128)(2,1)}), bf16[32,4,1024]{2,0,1:T(8,128)(2,1)S(1)}, u32[]{:S(2)}, u32[]{:S(2)}) async-start(bf16[32,4,1024]{2,0,1:T(8,128)(2,1)} %copy.84), calls=%async_computation.1 | async-start | bytes 524288 | tf_op jit(solution)/shard_map/all_to_all | solution.py:124
  124.7 8.4 collective-permute-start.2
  128.6 8.2 collective-permute-start
  143.0 8.3 collective-permute-start.2
  143.1 9.3 %collective-permute-start.3 = (f32[128,128]{1,0:T(8,128)S(1)}, f32[128,128]{1,0:T(8,128)S(1)}, u32[]{:S(2)}, u32[]{:S(2)}) collective-permute-start(f32[128,128]{1,0:T(8,128)S(1)} %get-tuple-element.1701), channel_id=1, source_target_pairs={{0,4},{4,8},{8,12},{12,16},{16,20},{20,24},{24,28},{28,32},{32,36}... | collective-permute-start | bytes 196616 | tf_op jit(solution)/shard_map/while/body/eval_jaxpr/ppermute | solution.py:15
  144.4 8.3 collective-permute-start
  157.8 9.0 collective-permute-start.2
  177.7 8.0 collective-permute-start.2
  177.8 8.6 collective-permute-start.3
  192.7 8.8 collective-permute-start.2
  192.8 8.7 collective-permute-start.3
  210.7 8.1 collective-permute-start.2
  216.8 8.1 collective-permute-start.1
  229.7 8.0 collective-permute-start.2
  229.7 8.7 collective-permute-start.3
  232.2 8.1 collective-permute-start.1
  245.0 9.0 collective-permute-start.2
  245.1 8.9 collective-permute-start.3
  261.7 8.4 collective-permute-start.2
  267.0 8.1 collective-permute-start.1
  279.8 8.6 collective-permute-start.2
  279.8 9.8 %collective-permute-start.3 = (f32[128,128]{1,0:T(8,128)S(1)}, f32[128,128]{1,0:T(8,128)S(1)}, u32[]{:S(2)}, u32[]{:S(2)}) collective-permute-start(f32[128,128]{1,0:T(8,128)S(1)} %get-tuple-element.1701), channel_id=1, source_target_pairs={{0,4},{4,8},{8,12},{12,16},{16,20},{20,24},{24,28},{28,32},{32,36}... | collective-permute-start | bytes 196616 | tf_op jit(solution)/shard_map/while/body/eval_jaxpr/ppermute | solution.py:15
  281.5 8.5 collective-permute-start
  282.3 8.0 collective-permute-start.1
  295.0 10.4 %collective-permute-start.2 = (f32[128,128]{1,0:T(8,128)S(1)}, f32[128,128]{1,0:T(8,128)S(1)}, u32[]{:S(2)}, u32[]{:S(2)}) collective-permute-start(f32[128,128]{1,0:T(8,128)S(1)} %get-tuple-element.1700), channel_id=1, source_target_pairs={{0,4},{4,8},{8,12},{12,16},{16,20},{20,24},{24,28},{28,32},{32,36}... | collective-permute-start | bytes 196616 | tf_op jit(solution)/shard_map/while/body/eval_jaxpr/ppermute | solution.py:15
  297.2 8.2 collective-permute-start.3
  331.1 8.6 collective-permute-start.3
  346.5 9.0 collective-permute-start.2
  380.8 10.3 %collective-permute-start.2 = (f32[128,128]{1,0:T(8,128)S(1)}, f32[128,128]{1,0:T(8,128)S(1)}, u32[]{:S(2)}, u32[]{:S(2)}) collective-permute-start(f32[128,128]{1,0:T(8,128)S(1)} %get-tuple-element.1700), channel_id=1, source_target_pairs={{0,4},{4,8},{8,12},{12,16},{16,20},{20,24},{24,28},{28,32},{32,36}... | collective-permute-start | bytes 196616 | tf_op jit(solution)/shard_map/while/body/eval_jaxpr/ppermute | solution.py:15
  381.0 10.1 %collective-permute-start.3 = (f32[128,128]{1,0:T(8,128)S(1)}, f32[128,128]{1,0:T(8,128)S(1)}, u32[]{:S(2)}, u32[]{:S(2)}) collective-permute-start(f32[128,128]{1,0:T(8,128)S(1)} %get-tuple-element.1701), channel_id=1, source_target_pairs={{0,4},{4,8},{8,12},{12,16},{16,20},{20,24},{24,28},{28,32},{32,36}... | collective-permute-start | bytes 196616 | tf_op jit(solution)/shard_map/while/body/eval_jaxpr/ppermute | solution.py:15
  394.9 12.0 %all-to-all-start.2 = ((bf16[4,32,1024]{2,1,0:T(8,128)(2,1)}), bf16[4,32,1024]{2,1,0:T(8,128)(2,1)S(1)}, u32[]{:S(2)}, u32[]{:S(2)}) async-start(bf16[4,32,1024]{2,1,0:T(8,128)(2,1)} %convert_element_type.172), calls=%async_computation.2 | async-start | bytes 524288 | tf_op jit(solution)/shard_map/all_to_all | solution.py:178
  409.6 91.3 %collective-permute-start.8 = (bf16[32,4096]{1,0:T(8,128)(2,1)}, bf16[32,4096]{1,0:T(8,128)(2,1)}, u32[]{:S(2)}, u32[]{:S(2)}) collective-permute-start(bf16[32,4096]{1,0:T(8,128)(2,1)} %fusion.122), channel_id=1, source_target_pairs={{64,0},{128,64},{192,128},{65,1},{129,65},{193,129},{66,2},{130,66... | collective-permute-start | bytes 786440 | tf_op jit(solution)/shard_map/ppermute | solution.py:21
  496.7 10.1 %all-to-all-start.3 = ((bf16[32,4,1024]{2,0,1:T(8,128)(2,1)}), bf16[32,4,1024]{2,0,1:T(8,128)(2,1)S(1)}, u32[]{:S(2)}, u32[]{:S(2)}) async-start(bf16[32,4,1024]{2,0,1:T(8,128)(2,1)} %get-tuple-element.1500), calls=%async_computation.3 | async-start | bytes 524288 | tf_op jit(solution)/shard_map/all_to_all | solution.py:123
  506.8 10.8 %all-to-all-start.4 = ((bf16[32,4,1024]{2,0,1:T(8,128)(2,1)}), bf16[32,4,1024]{2,0,1:T(8,128)(2,1)}, u32[]{:S(2)}, u32[]{:S(2)}) async-start(bf16[32,4,1024]{2,0,1:T(8,128)(2,1)} %bitcast.397), calls=%async_computation.4 | async-start | bytes 524288 | tf_op jit(solution)/shard_map/all_to_all | solution.py:124
  530.4 8.6 collective-permute-start.6
  533.1 8.1 collective-permute-start.4
  547.6 8.1 collective-permute-start.6
  547.7 8.7 collective-permute-start.7
  562.7 9.6 %collective-permute-start.6 = (f32[128,128]{1,0:T(8,128)S(1)}, f32[128,128]{1,0:T(8,128)S(1)}, u32[]{:S(2)}, u32[]{:S(2)}) collective-permute-start(f32[128,128]{1,0:T(8,128)S(1)} %get-tuple-element.1724), channel_id=1, source_target_pairs={{0,4},{4,8},{8,12},{12,16},{16,20},{20,24},{24,28},{28,32},{32,36}... | collective-permute-start | bytes 196616 | tf_op jit(solution)/shard_map/while/body/eval_jaxpr/ppermute | solution.py:15
  583.4 8.6 collective-permute-start.7
  598.3 8.1 collective-permute-start.6
  598.4 8.6 collective-permute-start.7
  615.6 8.7 collective-permute-start.6
  634.6 8.5 collective-permute-start.7
  636.8 8.3 collective-permute-start.5
  649.9 9.8 %collective-permute-start.6 = (f32[128,128]{1,0:T(8,128)S(1)}, f32[128,128]{1,0:T(8,128)S(1)}, u32[]{:S(2)}, u32[]{:S(2)}) collective-permute-start(f32[128,128]{1,0:T(8,128)S(1)} %get-tuple-element.1724), channel_id=1, source_target_pairs={{0,4},{4,8},{8,12},{12,16},{16,20},{20,24},{24,28},{28,32},{32,36}... | collective-permute-start | bytes 196616 | tf_op jit(solution)/shard_map/while/body/eval_jaxpr/ppermute | solution.py:15
  650.0 9.8 %collective-permute-start.7 = (f32[128,128]{1,0:T(8,128)S(1)}, f32[128,128]{1,0:T(8,128)S(1)}, u32[]{:S(2)}, u32[]{:S(2)}) collective-permute-start(f32[128,128]{1,0:T(8,128)S(1)} %get-tuple-element.1725), channel_id=1, source_target_pairs={{0,4},{4,8},{8,12},{12,16},{16,20},{20,24},{24,28},{28,32},{32,36}... | collective-permute-start | bytes 196616 | tf_op jit(solution)/shard_map/while/body/eval_jaxpr/ppermute | solution.py:15
  667.4 8.1 collective-permute-start.6
  670.0 8.0 collective-permute-start.7
  685.3 8.3 collective-permute-start.6
  685.4 8.9 collective-permute-start.7
  700.6 9.8 %collective-permute-start.6 = (f32[128,128]{1,0:T(8,128)S(1)}, f32[128,128]{1,0:T(8,128)S(1)}, u32[]{:S(2)}, u32[]{:S(2)}) collective-permute-start(f32[128,128]{1,0:T(8,128)S(1)} %get-tuple-element.1724), channel_id=1, source_target_pairs={{0,4},{4,8},{8,12},{12,16},{16,20},{20,24},{24,28},{28,32},{32,36}... | collective-permute-start | bytes 196616 | tf_op jit(solution)/shard_map/while/body/eval_jaxpr/ppermute | solution.py:15
  702.3 8.1 collective-permute-start.7
  720.2 8.0 collective-permute-start.6
  720.6 8.2 collective-permute-start.7
  735.9 8.0 collective-permute-start.6
  736.2 8.4 collective-permute-start.7
  752.5 8.8 collective-permute-start.6
  771.2 8.0 collective-permute-start.6
  771.6 8.3 collective-permute-start.7
  786.7 9.7 %collective-permute-start.6 = (f32[128,128]{1,0:T(8,128)S(1)}, f32[128,128]{1,0:T(8,128)S(1)}, u32[]{:S(2)}, u32[]{:S(2)}) collective-permute-start(f32[128,128]{1,0:T(8,128)S(1)} %get-tuple-element.1724), channel_id=1, source_target_pairs={{0,4},{4,8},{8,12},{12,16},{16,20},{20,24},{24,28},{28,32},{32,36}... | collective-permute-start | bytes 196616 | tf_op jit(solution)/shard_map/while/body/eval_jaxpr/ppermute | solution.py:15
  786.8 9.6 %collective-permute-start.7 = (f32[128,128]{1,0:T(8,128)S(1)}, f32[128,128]{1,0:T(8,128)S(1)}, u32[]{:S(2)}, u32[]{:S(2)}) collective-permute-start(f32[128,128]{1,0:T(8,128)S(1)} %get-tuple-element.1725), channel_id=1, source_target_pairs={{0,4},{4,8},{8,12},{12,16},{16,20},{20,24},{24,28},{28,32},{32,36}... | collective-permute-start | bytes 196616 | tf_op jit(solution)/shard_map/while/body/eval_jaxpr/ppermute | solution.py:15
  800.3 10.1 %all-to-all-start.5 = ((bf16[4,32,1024]{2,1,0:T(8,128)(2,1)}), bf16[4,32,1024]{2,1,0:T(8,128)(2,1)S(1)}, u32[]{:S(2)}, u32[]{:S(2)}) async-start(bf16[4,32,1024]{2,1,0:T(8,128)(2,1)} %convert_element_type.193), calls=%async_computation.5 | async-start | bytes 524288 | tf_op jit(solution)/shard_map/all_to_all | solution.py:178
  (82 other events, 3383.6 us)
